TPU v7x, 32 devices: a whole 2x2x4 slice. The times are simulated.
32 devices in a mesh: pop: 8 (over z, x), grp: 4 (over y, core).
Axes of the slice: x: 2, y: 2, z: 4, core: 2. Of those that a mesh axis runs over, the one named last changes fastest.
Arguments:
- actions: bfloat16 [16384, 1024], P(('pop', 'grp')), may hold values from -6 to 6
- elite_mask: int32 [16384], P(('pop', 'grp')), may hold values from 0 to 1, as said below
- init_state: float32 [256], replicated, may hold values from -6 to 6
- w_state: bfloat16 [256, 256], replicated, may hold values from -0.375 to 0.375
- w_action: bfloat16 [32, 256], replicated, may hold values from -1 to 1
- bias: float32 [256], replicated, may hold values from -3 to 3
- w_out: bfloat16 [256, 256], replicated, may hold values from -0.375 to 0.375
- reward_vec: float32 [256], replicated, may hold values from -0.375 to 0.375
Outputs:
- new_mean: float32 [1024], replicated
- covariance: float32 [1024, 1024], P('pop')
- returns: float32 [16384], P(('pop', 'grp'))
Inputs may be any that keep to these rules, and one draw needn't show every extreme that they name: `elite_mask`: each aligned block of 512 candidates (the candidates of one device) holds at least one elite.
All inputs are finite; a program needn't handle non-finite values.
Results may differ from a plain program's by a relative error of at most 0.0063.
Values sent between devices are 32-bit elements; how exact they have to be, the bound alone decides.
No kernel may reach another device: no remote copies, remote signals or barrier semaphores. Data moves between devices by JAX's collectives and lax.ppermute only.
A program may use at most 64 MiB of HBM per device.

v0:
```python
import jax
import jax.numpy as jnp
from jax import lax
from jax.sharding import PartitionSpec as P

ACT = 32
STEPS = 32
STATE = 256


def on_device(actions, elite_mask, init_state, w_state, w_action, bias, w_out, reward_vec):
    cand_rows = actions.shape[0]
    width_all = actions.shape[1]
    weight = elite_mask.astype(jnp.float32)
    weight_b = weight.astype(jnp.bfloat16)
    local_sums = jnp.dot(weight_b[None, :], actions, preferred_element_type=jnp.float32)[0]
    local_count = jnp.sum(weight)
    sums, count = lax.psum((local_sums, local_count), ("pop", "grp"))
    new_mean = sums / count
    masked = actions * weight_b[:, None]
    pop_count = lax.axis_size("pop")
    own_rows = width_all // pop_count
    pop_index = lax.axis_index("pop")
    first_row = pop_index * own_rows
    slab = lax.psum_scatter(
        lax.dot_general(
            masked, actions, (((0,), (0,)), ((), ())), preferred_element_type=jnp.float32
        ),
        "pop",
        scatter_dimension=0,
        tiled=True,
    )
    mine = lax.psum(slab, "grp")
    mean_rows = lax.dynamic_slice_in_dim(new_mean, first_row, own_rows, 0)
    covariance = mine / count - mean_rows[:, None] * new_mean[None, :]
    per_step = jnp.transpose(actions.reshape(cand_rows, STEPS, ACT), (1, 0, 2))
    start_state = jnp.broadcast_to(init_state[None, :], (cand_rows, STATE))

    def advance(carry, action_now):
        state, total = carry
        state_b = state.astype(jnp.bfloat16)
        pre = jnp.dot(state_b, w_state, preferred_element_type=jnp.float32)
        pre = pre + jnp.dot(action_now, w_action, preferred_element_type=jnp.float32) + bias
        hidden = jnp.tanh(pre).astype(jnp.bfloat16)
        state = 0.9 * state + jnp.dot(hidden, w_out, preferred_element_type=jnp.float32)
        total = total + jnp.sum(state * reward_vec[None, :], axis=1)
        return ((state, total), None)

    (final_state, total), unused = lax.scan(
        advance, (start_state, jnp.zeros((cand_rows,), jnp.float32)), per_step
    )
    returns = total / STEPS
    return (new_mean, covariance, returns)


def solution(mesh):
    placed = (P(("pop", "grp"), None), P(("pop", "grp")), P(), P(), P(), P(), P(), P())
    return jax.shard_map(
        on_device,
        mesh=mesh,
        in_specs=placed,
        out_specs=(P(), P("pop", None), P(("pop", "grp"))),
        check_vma=False,
    )
```

profile of v0, /device:TPU:0, one launch (start us, length us, event | category | flops | bytes accessed | tf_op | source)
XLA Modules:
  0.0 149.3 jit_solution(13293157726745126717)
XLA Ops:
  7.2 0.7 convert_convert_fusion
  7.9 5.0 %fusion.12 = f32[1024,1024]{1,0:T(8,128)} fusion(bf16[512,1024]{1,0:T(8,128)(2,1)} %param.10, bf16[512]{0:T(512)(128)(2,1)S(1)} %convert_convert_fusion), kind=kOutput, calls=%fused_computation.13 | convolution fusion | flops 1074266112 | bytes 5243904 | tf_op jit(solution)/shard_map/dot_general | solution.py:26
  13.0 0.5 copy.11
  13.9 34.1 %while.13 = (s32[]{:T(128)}, f32[512,256]{0,1:T(8,128)S(1)}, f32[512]{0:T(512)S(1)}, bf16[256,256]{1,0:T(8,128)(2,1)S(1)}, bf16[32,512,32]{1,2,0:T(8,128)(2,1)S(...) while((s32[]{:T(128)}, f32[512,256]{0,1:T(8,128)S(1)}, ...), condition=%wide.region_7.8_spmd.clone, body=%wide.region_5.7_spmd.clone.sunk | while | flops 143655424 | bytes 2943107 | solution.py:49
  13.9 0.3 fusion.35
  14.1 0.8 multiply_reduce_fusion.2
  15.2 0.8 multiply_reduce_fusion.2
  16.3 0.8 multiply_reduce_fusion.2
  17.3 0.8 multiply_reduce_fusion.2
  18.1 0.3 fusion.35
  18.4 0.8 multiply_reduce_fusion.2
  19.2 0.3 fusion.35
  19.5 0.8 multiply_reduce_fusion.2
  20.3 0.3 fusion.35
  20.5 0.8 multiply_reduce_fusion.2
  21.6 0.8 multiply_reduce_fusion.2
  22.7 0.8 multiply_reduce_fusion.2
  23.7 0.8 multiply_reduce_fusion.2
  24.5 0.3 fusion.35
  24.8 0.8 multiply_reduce_fusion.2
  25.9 0.8 multiply_reduce_fusion.2
  26.9 0.8 multiply_reduce_fusion.2
  28.0 0.8 multiply_reduce_fusion.2
  29.1 0.8 multiply_reduce_fusion.2
  30.1 0.8 multiply_reduce_fusion.2
  31.2 0.8 multiply_reduce_fusion.2
  32.2 0.8 multiply_reduce_fusion.2
  33.3 0.8 multiply_reduce_fusion.2
  34.4 0.8 multiply_reduce_fusion.2
  35.4 0.8 multiply_reduce_fusion.2
  36.5 0.8 multiply_reduce_fusion.2
  37.6 0.8 multiply_reduce_fusion.2
  38.6 0.8 multiply_reduce_fusion.2
  39.7 0.8 multiply_reduce_fusion.2
  40.8 0.8 multiply_reduce_fusion.2
  41.8 0.8 multiply_reduce_fusion.2
  42.9 0.8 multiply_reduce_fusion.2
  44.0 0.8 multiply_reduce_fusion.2
  45.0 0.8 multiply_reduce_fusion.2
  46.1 0.8 multiply_reduce_fusion.2
  47.2 0.8 multiply_reduce_fusion.2
  48.0 0.6 convert_reduce_fusion
  48.8 42.3 %all-reduce = (f32[1024]{0:T(1024)S(1)}, f32[]{:T(128)}) all-reduce(f32[1024]{0:T(1024)S(1)} %bitcast.26, f32[]{:T(128)} %convert_reduce_fusion), channel_id=1, replica_groups=mesh['pop'=8,'grp'=4] {'pop','grp'}, use_global_device_ids=true, to_apply=%region_0.0 | all-reduce | flops 1025 | bytes 8200 | tf_op jit(solution)/shard_map/psum | solution.py:18
  91.1 13.3 %reduce-scatter.2.cloned.1.call-done = f32[128,1024]{1,0:T(8,128)} async-done(((f32[1024,1024]{1,0:T(8,128)}), f32[128,1024]{1,0:T(8,128)}) %reduce-scatter.2.cloned.1.call-update) | async-done | bytes 524304 | tf_op jit(solution)/shard_map/reduce_scatter | solution.py:25
  104.5 0.6 broadcast_divide_fusion
  105.2 0.6 broadcast_multiply_fusion
  105.8 34.1 %all-reduce.3.cloned.1.call-done = f32[128,1024]{1,0:T(8,128)} async-done(((f32[128,1024]{1,0:T(8,128)}), f32[128,1024]{1,0:T(8,128)}) %all-reduce.3.cloned.1.call-update) | async-done | bytes 524304 | tf_op jit(solution)/shard_map/psum | solution.py:33
  139.9 2.6 %multiply_subtract_fusion = f32[128,1024]{1,0:T(8,128)} fusion(f32[128,1024]{1,0:T(8,128)} %all-reduce.3.cloned.1.call-done, f32[1024]{0:T(1024)S(1)} %broadcast_divide_fusion, f32[128]{0:T(128)S(1)} %dynamic_slice.7, f32[]{:T(128)} %get-tuple-element.109), kind=kLoop, calls=%fused_computation.15 | loop fusion | flops 393216 | bytes 1053188 | tf_op jit(solution)/shard_map/sub | solution.py:35
  (86 shorter events, 8.3 us)
Async XLA Ops:
  7.2 97.3 %reduce-scatter.2.cloned.1.call-start = ((), (), s32[]{:S(2)}) async-start(), calls=%async_computation.1 | async-start | bytes 4718592 | tf_op jit(solution)/shard_map/reduce_scatter | solution.py:25
  7.9 5.1 %copy-start = (bf16[512,1024]{1,0:T(8,128)(2,1)S(1)}, bf16[512,1024]{1,0:T(8,128)(2,1)}, u32[]{:S(2)}) copy-start(bf16[512,1024]{1,0:T(8,128)(2,1)} %param.10) | copy-start | bytes 3145732
  12.9 0.7 copy-start.8
  12.9 0.9 copy-start.1
  12.9 1.0 copy-start.2
  12.9 1.0 copy-start.3
  12.9 1.0 copy-start.4
  12.9 1.0 copy-start.5
  12.9 127.0 %all-reduce.3.cloned.1.call-start = ((), (), s32[]{:S(2)}) async-start(), calls=%async_computation.2 | async-start | bytes 1048576 | tf_op jit(solution)/shard_map/psum | solution.py:33
  13.9 34.1 %copy-start.7 = (s32[512]{0:T(512)S(1)}, s32[512]{0:T(512)}, u32[]{:S(2)}) copy-start(s32[512]{0:T(512)} %param.11) | copy-start | bytes 6148
  105.1 37.3 %copy-start.6 = (f32[1024]{0:T(1024)}, f32[1024]{0:T(1024)S(1)}, u32[]{:S(2)}) copy-start(f32[1024]{0:T(1024)S(1)} %broadcast_divide_fusion) | copy-start | bytes 12292
Sparse Core Ops, SparseCore 0:
  13.0 91.3 reduce-scatter.1
  106.8 33.0 all-reduce.2
where the time goes:
time: 150 us; the launch traced here: 149 us
  waiting for transfers between devices  47.5 us (32%)
  blocking collectives  42.3 us (28%)
  matrix products  38.2 us (25%)
  between operations  14.2 us (9%)
  other arithmetic  5.48 us (4%)
    psum x1, blocking collectives, on_device(): sums, count = lax.psum((local_sums, local_count), ('pop', 'grp'))  42.3 us
    psum x1, waiting for transfers between devices, on_device(): mine = lax.psum(slab, 'grp')  34.1 us
    dot_general x32, matrix products, advance(): jnp.dot(hidden, w_out, preferred_element_type=jnp.float32)  24.6 us
    reduce_scatter x1, waiting for transfers between devices, on_device(): lax.psum_scatter(lax.dot_general(masked, actions, (((0,), (0,)), ((), ())...  13.3 us
    dot_general x32, matrix products, advance(): pre = jnp.dot(state_b, w_state, preferred_element_type=jnp.float32)  8.45 us
    dot_general x1, matrix products, on_device(): lax.dot_general(masked, actions, (((0,), (0,)), ((), ())), preferred_elem...  4.96 us
  transfers between devices with their start and end apart: 2, of which 2 were waited for; matrix products, arithmetic and copies ran while one was open for 24% of the time, Pallas kernels for 0%

commit v1 on v0

--- a/solution.py
+++ b/solution.py
@@ -6,6 +6,15 @@
 ACT = 32
 STEPS = 32
 STATE = 256
+
+
+def sum_by_hops(x, axis):
+    size = lax.axis_size(axis)
+    total, far = (x, 1)
+    while far < size:
+        total = total + lax.ppermute(total, axis, [(i, i ^ far) for i in range(size)])
+        far = 2 * far
+    return total
 
 
 def on_device(actions, elite_mask, init_state, w_state, w_action, bias, w_out, reward_vec):
@@ -30,7 +39,7 @@
         scatter_dimension=0,
         tiled=True,
     )
-    mine = lax.psum(slab, "grp")
+    mine = sum_by_hops(slab, "grp")
     mean_rows = lax.dynamic_slice_in_dim(new_mean, first_row, own_rows, 0)
     covariance = mine / count - mean_rows[:, None] * new_mean[None, :]
     per_step = jnp.transpose(actions.reshape(cand_rows, STEPS, ACT), (1, 0, 2))

time: 150 us -> 197 us (1.31)
  waiting for transfers between devices: 47.5 us -> 90.7 us
  blocking collectives: 42.3 us -> 45.2 us
    reduce_scatter x1, waiting for transfers between devices: 13.3 us -> 90.6 us  [on_device(): lax.psum_scatter(lax.dot_general(masked, actions, (((0,), (0,)), ((), ())...]
    psum x1 -> x0, waiting for transfers between devices: 34.1 us -> none  [on_device(): mine = lax.psum(slab, 'grp')]
    psum x1, blocking collectives: 42.3 us -> 45.2 us  [on_device(): sums, count = lax.psum((local_sums, local_count), ('pop', 'grp'))]
  transfers between devices with their start and end apart: 2 -> 3, of which waited for: 2 -> 1; matrix products, arithmetic and copies ran while one was open for 24% -> 18% of each run, Pallas kernels for 0% -> 0%
where the time goes in v1:
time: 197 us
  waiting for transfers between devices  90.7 us (46%)
  blocking collectives  45.2 us (23%)
  matrix products  38.2 us (19%)
  between operations  14.2 us (7%)
  other arithmetic  5.56 us (3%)
    reduce_scatter x1, waiting for transfers between devices, on_device(): lax.psum_scatter(lax.dot_general(masked, actions, (((0,), (0,)), ((), ())...  90.6 us
    psum x1, blocking collectives, on_device(): sums, count = lax.psum((local_sums, local_count), ('pop', 'grp'))  45.2 us
    dot_general x32, matrix products, advance(): jnp.dot(hidden, w_out, preferred_element_type=jnp.float32)  24.6 us
    dot_general x32, matrix products, advance(): pre = jnp.dot(state_b, w_state, preferred_element_type=jnp.float32)  8.45 us
    dot_general x1, matrix products, on_device(): lax.dot_general(masked, actions, (((0,), (0,)), ((), ())), preferred_elem...  4.95 us
  transfers between devices with their start and end apart: 3, of which 1 were waited for; matrix products, arithmetic and copies ran while one was open for 18% of the time, Pallas kernels for 0%

profile of v1, /device:TPU:0, one launch (start us, length us, event | category | flops | bytes accessed | tf_op | source)
XLA Modules:
  0.0 196.8 jit_solution(16101372539195447534)
XLA Ops:
  7.2 0.7 convert_convert_fusion
  7.9 4.9 %fusion.12 = f32[1024,1024]{1,0:T(8,128)} fusion(bf16[512,1024]{1,0:T(8,128)(2,1)} %param.10, bf16[512]{0:T(512)(128)(2,1)S(1)} %convert_convert_fusion), kind=kOutput, calls=%fused_computation.13 | convolution fusion | flops 1074266112 | bytes 5243904 | tf_op jit(solution)/shard_map/dot_general | solution.py:35
  12.9 0.5 copy.11
  13.5 90.6 %reduce-scatter.2.cloned.1.call-done = f32[128,1024]{1,0:T(8,128)} async-done(((f32[1024,1024]{1,0:T(8,128)}), f32[128,1024]{1,0:T(8,128)}) %reduce-scatter.2.cloned.1.call-update) | async-done | bytes 524304 | tf_op jit(solution)/shard_map/reduce_scatter | solution.py:34
  104.3 34.1 %while.13 = (s32[]{:T(128)}, f32[512,256]{0,1:T(8,128)S(1)}, f32[512]{0:T(512)S(1)}, bf16[256,256]{1,0:T(8,128)(2,1)S(1)}, bf16[32,512,32]{1,2,0:T(8,128)(2,1)S(...) while((s32[]{:T(128)}, f32[512,256]{0,1:T(8,128)S(1)}, ...), condition=%wide.region_6.7_spmd.clone, body=%wide.region_4.6_spmd.clone.sunk | while | flops 143655424 | bytes 2943107 | solution.py:58
  104.6 0.8 multiply_reduce_fusion.2
  105.4 0.3 fusion.35
  105.6 0.8 multiply_reduce_fusion.2
  106.4 0.3 fusion.35
  106.7 0.8 multiply_reduce_fusion.2
  107.5 0.3 fusion.35
  107.8 0.8 multiply_reduce_fusion.2
  108.8 0.8 multiply_reduce_fusion.2
  109.9 0.8 multiply_reduce_fusion.2
  111.0 0.8 multiply_reduce_fusion.2
  111.8 0.3 fusion.35
  112.0 0.8 multiply_reduce_fusion.2
  113.1 0.8 multiply_reduce_fusion.2
  114.2 0.8 multiply_reduce_fusion.2
  115.2 0.8 multiply_reduce_fusion.2
  116.3 0.8 multiply_reduce_fusion.2
  117.4 0.8 multiply_reduce_fusion.2
  118.4 0.8 multiply_reduce_fusion.2
  119.5 0.8 multiply_reduce_fusion.2
  120.6 0.8 multiply_reduce_fusion.2
  121.6 0.8 multiply_reduce_fusion.2
  122.7 0.8 multiply_reduce_fusion.2
  123.7 0.8 multiply_reduce_fusion.2
  124.8 0.8 multiply_reduce_fusion.2
  125.9 0.8 multiply_reduce_fusion.2
  126.9 0.8 multiply_reduce_fusion.2
  128.0 0.8 multiply_reduce_fusion.2
  129.1 0.8 multiply_reduce_fusion.2
  130.1 0.8 multiply_reduce_fusion.2
  131.2 0.8 multiply_reduce_fusion.2
  132.3 0.8 multiply_reduce_fusion.2
  133.3 0.8 multiply_reduce_fusion.2
  134.4 0.8 multiply_reduce_fusion.2
  135.5 0.8 multiply_reduce_fusion.2
  136.5 0.8 multiply_reduce_fusion.2
  137.6 0.8 multiply_reduce_fusion.2
  138.7 1.3 add.35
  139.9 1.5 collective-permute-start.1
  141.5 0.6 convert_reduce_fusion
  142.1 45.2 %all-reduce = (f32[1024]{0:T(1024)S(1)}, f32[]{:T(128)}) all-reduce(f32[1024]{0:T(1024)S(1)} %bitcast.26, f32[]{:T(128)} %convert_reduce_fusion), channel_id=1, replica_groups=mesh['pop'=8,'grp'=4] {'pop','grp'}, use_global_device_ids=true, to_apply=%region_0.0 | all-reduce | flops 1025 | bytes 8200 | tf_op jit(solution)/shard_map/psum | solution.py:27
  187.2 0.6 broadcast_divide_fusion
  187.9 0.6 broadcast_multiply_fusion
  188.5 1.5 multiply_subtract_fusion
  (88 shorter events, 8.3 us)
Async XLA Ops:
  7.2 97.0 %reduce-scatter.2.cloned.1.call-start = ((), (), s32[]{:S(2)}) async-start(), calls=%async_computation.1 | async-start | bytes 4718592 | tf_op jit(solution)/shard_map/reduce_scatter | solution.py:34
  7.9 5.0 %copy-start = (bf16[512,1024]{1,0:T(8,128)(2,1)S(1)}, bf16[512,1024]{1,0:T(8,128)(2,1)}, u32[]{:S(2)}) copy-start(bf16[512,1024]{1,0:T(8,128)(2,1)} %param.10) | copy-start | bytes 3145732
  12.8 91.3 %copy-start.8 = (f32[256]{0:T(256)S(1)}, f32[256]{0:T(256)}, u32[]{:S(2)}) copy-start(f32[256]{0:T(256)} %param.12) | copy-start | bytes 3076
  12.9 91.4 %copy-start.1 = (bf16[256,256]{1,0:T(8,128)(2,1)S(1)}, bf16[256,256]{1,0:T(8,128)(2,1)}, u32[]{:S(2)}) copy-start(bf16[256,256]{1,0:T(8,128)(2,1)} %param.13) | copy-start | bytes 393220
  12.9 91.4 %copy-start.2 = (bf16[256,256]{1,0:T(8,128)(2,1)S(1)}, bf16[256,256]{1,0:T(8,128)(2,1)}, u32[]{:S(2)}) copy-start(bf16[256,256]{1,0:T(8,128)(2,1)} %param.16) | copy-start | bytes 393220
  12.9 91.4 %copy-start.3 = (bf16[32,256]{1,0:T(8,128)(2,1)S(1)}, bf16[32,256]{1,0:T(8,128)(2,1)}, u32[]{:S(2)}) copy-start(bf16[32,256]{1,0:T(8,128)(2,1)} %param.14) | copy-start | bytes 49156
  12.9 91.4 %copy-start.4 = (f32[256]{0:T(256)S(1)}, f32[256]{0:T(256)}, u32[]{:S(2)}) copy-start(f32[256]{0:T(256)} %param.15) | copy-start | bytes 3076
  12.9 91.4 %copy-start.5 = (f32[256]{0:T(256)S(1)}, f32[256]{0:T(256)}, u32[]{:S(2)}) copy-start(f32[256]{0:T(256)} %param.17) | copy-start | bytes 3076
  104.1 34.5 %collective-permute-start = (f32[128,1024]{1,0:T(8,128)}, f32[128,1024]{1,0:T(8,128)}, u32[]{:S(2)}, u32[]{:S(2)}) collective-permute-start(f32[128,1024]{1,0:T(8,128)} %reduce-scatter.2.cloned.1.call-done), channel_id=1, source_target_pairs={{0,1},{1,0},{2,3},{3,2},{4,5},{5,4},{6,7},{7,6},{8,9},{9,8},{10,11... | collective-permute-start | bytes 1572872 | tf_op jit(solution)/shard_map/ppermute | solution.py:15
  104.3 37.2 %copy-start.7 = (s32[512]{0:T(512)S(1)}, s32[512]{0:T(512)}, u32[]{:S(2)}) copy-start(s32[512]{0:T(512)} %param.11) | copy-start | bytes 6148
  139.9 48.6 %collective-permute-start.1 = (f32[128,1024]{1,0:T(8,128)S(1)}, f32[128,1024]{1,0:T(8,128)S(1)}, u32[]{:S(2)}, u32[]{:S(2)}) collective-permute-start(f32[128,1024]{1,0:T(8,128)S(1)} %add.35), channel_id=1, source_target_pairs={{0,2},{1,3},{2,0},{3,1},{4,6},{5,7},{6,4},{7,5},{8,10},{9,11},{10,... | collective-permute-start | bytes 1572872 | tf_op jit(solution)/shard_map/ppermute | solution.py:15
  187.8 2.1 %copy-start.6 = (f32[1024]{0:T(1024)}, f32[1024]{0:T(1024)S(1)}, u32[]{:S(2)}) copy-start(f32[1024]{0:T(1024)S(1)} %broadcast_divide_fusion) | copy-start | bytes 12292
Sparse Core Ops, SparseCore 0:
  13.0 91.0 reduce-scatter.1
